TPU v7x, 128 devices: a whole 4x4x4 slice. The times are simulated.
128 devices in a mesh: rep: 16 (over x, y), exp: 8 (over z, core).
Axes of the slice: x: 4, y: 4, z: 4, core: 2. Of those that a mesh axis runs over, the one named last changes fastest.
Arguments:
- hidden: bfloat16 [16384, 4096], P(('rep', 'exp')), may hold values from -6 to 6
- parents: int32 [16384], P(('rep', 'exp')), may hold values from 0 to 1023
- routes: int32 [16384, 8], P(('rep', 'exp')), may hold values from 0 to 127, all different within a row; in each aligned block of 128 rows (0 to 127, 128 to 255, ...) at most 10 rows name the same one
- gates: float32 [16384, 8], P(('rep', 'exp')), may hold values from 0.05 to 1
- counts: int32 [128], P(('rep', 'exp')), may hold values from 64 to 128, as said below
- norm_gain: float32 [4096], replicated, may hold values from 0.1 to 1.9
- w_gate: bfloat16 [128, 4096, 768], P(('rep', 'exp')), may hold values from -0.09375 to 0.09375
- w_up: bfloat16 [128, 4096, 768], P(('rep', 'exp')), may hold values from -0.09375 to 0.09375
- w_down: bfloat16 [128, 768, 4096], P(('rep', 'exp')), may hold values from -0.21875 to 0.21875
Outputs:
- mixed: bfloat16 [16384, 4096], P(('rep', 'exp'))
Inputs may be any that keep to these rules, and one draw needn't show every extreme that they name: `routes`: in the rows of one device no expert is named more than 10 times. `counts`: some device has all of its rows live.
All inputs are finite; a program needn't handle non-finite values.
Results may differ from a plain program's by a relative error of at most 0.0071.
Values may be sent and summed in bfloat16 or wider, within the bound.
A program may use at most 128 MiB of HBM per device.

v0:
```python
import jax
import jax.numpy as jnp
from jax import lax
from jax.sharding import PartitionSpec as P


def run_expert(arrived, w_gate, w_up, w_down):
    gate_val = jnp.dot(arrived, w_gate[0], preferred_element_type=jnp.float32)
    up_val = jnp.dot(arrived, w_up[0], preferred_element_type=jnp.float32)
    act = (jax.nn.silu(gate_val) * up_val).astype(jnp.bfloat16)
    return jnp.dot(act, w_down[0], preferred_element_type=jnp.float32).astype(jnp.bfloat16)


def shards(hidden, parents, routes, gates, counts, norm_gain, w_gate, w_up, w_down):
    rows = hidden.shape[0]
    width = hidden.shape[1]
    top = routes.shape[1]
    n_rep = lax.axis_size("rep")
    n_exp = lax.axis_size("exp")
    n_dev = n_rep * n_exp
    cap = rows * top // n_dev + 2
    column = lax.axis_index("exp")
    micro = rows * n_exp
    per_expert = cap * n_exp
    slots = n_rep * per_expert
    live = jnp.arange(rows, dtype=jnp.int32) < counts[0]
    weights = gates / jnp.sum(gates, axis=1, keepdims=True) * live[:, None].astype(jnp.float32)
    flat = routes.reshape(-1)
    live_slot = jnp.repeat(live, top)
    onehot = (
        (flat[:, None] == jnp.arange(n_dev, dtype=jnp.int32)[None, :]) & live_slot[:, None]
    ).astype(jnp.int32)
    before = jnp.cumsum(onehot, axis=0) - onehot
    rank = jnp.sum(before * onehot, axis=1)
    code = jnp.where(live_slot, flat, -1)
    ints = jnp.concatenate(
        [code.reshape(rows, top), rank.reshape(rows, top), parents[:, None]], axis=1
    )
    group = lax.all_gather(hidden, "exp", axis=0, tiled=True)
    ints_all = lax.all_gather(ints, "exp", axis=0, tiled=True)
    w_all = lax.all_gather(weights, "exp", axis=0, tiled=True)
    code_all = ints_all[:, :top]
    rank_all = ints_all[:, top : 2 * top]
    parent_all = ints_all[:, 2 * top]
    mine = (code_all >= 0) & (code_all % n_exp == column)
    owner = (jnp.arange(micro, dtype=jnp.int32) // rows)[:, None]
    dest = code_all // n_exp * per_expert + owner * cap + rank_all
    dest = jnp.where(mine, dest, slots).reshape(-1)
    row_id = jnp.broadcast_to(jnp.arange(micro, dtype=jnp.int32)[:, None], (micro, top)).reshape(-1)
    src_row = jnp.zeros((slots,), jnp.int32).at[dest].set(row_id, mode="drop")
    filled = jnp.zeros((slots,), jnp.bool_).at[dest].set(True, mode="drop")
    slot_w = jnp.zeros((slots,), jnp.float32).at[dest].set(w_all.reshape(-1), mode="drop")
    picked = jnp.take(group, jnp.take(parent_all, src_row), axis=0).astype(jnp.float32)
    scale = lax.rsqrt(jnp.mean(picked * picked, axis=1, keepdims=True) + 1e-06)
    normed = (picked * scale * norm_gain).astype(jnp.bfloat16)
    outgoing = jnp.where(filled[:, None], normed, jnp.zeros((), jnp.bfloat16))
    arrived = lax.all_to_all(outgoing, "rep", split_axis=0, concat_axis=0, tiled=True)
    results = run_expert(arrived, w_gate, w_up, w_down)
    returned = lax.all_to_all(results, "rep", split_axis=0, concat_axis=0, tiled=True)
    contrib = slot_w[:, None] * returned.astype(jnp.float32)
    target = jnp.where(filled, src_row, micro)
    partial = jnp.zeros((micro, width), jnp.float32).at[target].add(contrib, mode="drop")
    mixed = lax.psum_scatter(partial.astype(jnp.bfloat16), "exp", scatter_dimension=0, tiled=True)
    return mixed


def solution(mesh):
    placed = (
        P(("rep", "exp"), None),
        P(("rep", "exp")),
        P(("rep", "exp"), None),
        P(("rep", "exp"), None),
        P(("rep", "exp")),
        P(),
        P(("rep", "exp"), None, None),
        P(("rep", "exp"), None, None),
        P(("rep", "exp"), None, None),
    )
    return jax.shard_map(
        shards, mesh=mesh, in_specs=placed, out_specs=P(("rep", "exp"), None), check_vma=False
    )
```

profile of v0, /device:TPU:1, one launch (start us, length us, event | category | flops | bytes accessed | tf_op | source)
XLA Modules:
  0.0 590.4 jit_solution(2126128571061677138)
XLA Ops:
  6.5 0.0 all-gather.2.cloned.1.call-start
  6.5 0.7 all-gather.2.cloned.1.call-update
  7.3 0.8 copy.28
  8.0 0.1 eq.37
  8.1 0.1 eq.33
  8.9 0.1 broadcast_in_dim.94.clone
  9.0 0.1 and.55
  9.1 0.1 copy.31
  9.2 0.3 fusion.17
  9.7 0.1 copy.32
  9.8 0.5 fusion.16
  10.3 0.1 reshape.149
  10.4 0.7 broadcast_select_fusion
  11.1 0.7 pad_add_fusion
  11.8 15.3 %all_gather.9 = s32[1024,17]{0,1:T(8,128)S(1)} all-gather(s32[128,17]{0,1:T(8,128)S(1)} %pad_add_fusion), channel_id=1, replica_groups=mesh['rep'=16,'exp'=8] {'exp'}, dimensions={0}, use_global_device_ids=true | all-gather | bytes 78336 | tf_op jit(solution)/shard_map/all_gather | solution.py:40
  27.1 0.2 copy.34
  27.3 0.3 reshape.150
  27.7 34.6 %scatter_custom_fusion = pred[1280]{0:T(1024)(128)(4,1)S(1)} fusion(s32[8192]{0:T(1024)S(1)} %bitcast.48, pred[8192]{0:T(1024)(128)(4,1)S(1)} %broadcast.149, pred[]{:T(512)} %constant.90.clone.1), kind=kCustom, calls=%fused_computation.72 | custom fusion | bytes 1281 | tf_op jit(solution)/shard_map/scatter | solution.py:51
  62.3 0.1 broadcast_in_dim.105
  62.4 0.3 reshape.182
  62.7 30.9 %scatter_custom_fusion.1 = s32[1280]{0:T(1024)S(1)} fusion(s32[8192]{0:T(1024)S(1)} %bitcast.49, s32[8192]{0:T(1024)S(1)} %reshape.182, s32[]{:T(128)} %constant.93.clone.1), kind=kCustom, calls=%fused_computation.69 | custom fusion | bytes 5124 | tf_op jit(solution)/shard_map/scatter | solution.py:50
  93.6 5.0 gather_fusion
  98.6 0.1 broadcast_in_dim.109
  98.7 0.0 all-gather.2.cloned.1.call-done
  98.7 23.2 %gather_fusion.1 = bf16[1280,4096]{1,0:T(8,128)(2,1)} fusion(bf16[1024,4096]{1,0:T(8,128)(2,1)} %all-gather.2.cloned.1.call-done, s32[2048]{0:T(1024)S(1)} %pad_clamp_fusion), kind=kCustom, calls=%fused_computation.1 | custom fusion | bytes 20976640 | tf_op jit(solution)/shard_map/jit(_take)/gather | solution.py:53
  121.9 6.9 %multiply_reduce_fusion = f32[1280]{0:T(1024)S(1)} fusion(bf16[1280,4096]{1,0:T(8,128)(2,1)} %gather_fusion.1, pred[1280]{0:T(1024)(128)(4,1)S(1)} %get-tuple-element.5), kind=kLoop, calls=%fused_computation.9 | loop fusion | flops 20970240 | bytes 10492160 | tf_op jit(solution)/shard_map/reduce_sum | solution.py:54
  128.8 0.1 rsqrt.12
  128.9 0.0 copy-done
  128.9 9.0 %fusion.1 = bf16[16,80,4096]{2,1,0:T(8,128)(2,1)S(1)} fusion(f32[4096]{0:T(1024)S(1)} %copy-done, f32[16,80]{1,0:T(8,128)S(1)} %rsqrt.12, bf16[16,80,4096]{2,1,0:T(8,128)(2,1)} %bitcast.44, pred[16,80]{1,0:T(8,128)(4,1)S(1)} %broadcast_in_dim.109, pred[16,80]{1,0:T(8,128)(4,1)S(1)} %broadcast_in_dim.105), kind=kLoop, calls=%fused_computation.11 | loop fusion | flops 31457280 | bytes 20995584 | tf_op jit(solution)/shard_map/jit(_where)/select_n | solution.py:56
  138.0 0.0 slice-start
  138.0 0.0 slice-start.2
  138.0 123.9 %all_to_all.18 = bf16[16,80,4096]{2,1,0:T(8,128)(2,1)S(1)} all-to-all(bf16[16,80,4096]{2,1,0:T(8,128)(2,1)S(1)} %fusion.1), channel_id=1, replica_groups=mesh['rep'=16,'exp'=8] {'rep'}, dimensions={0} | all-to-all | bytes 20971520 | tf_op jit(solution)/shard_map/all_to_all | solution.py:57
  261.9 11.8 %fusion.7 = f32[1280,768]{1,0:T(8,128)} fusion(bf16[1280,4096]{1,0:T(8,128)(2,1)S(1)} %bitcast.46, bf16[1,4096,768]{2,1,0:T(8,128)(2,1)} %param.15), kind=kOutput, calls=%fused_computation.17 | convolution fusion | flops 8053063680 | bytes 20709376 | tf_op jit(solution)/shard_map/dot_general | solution.py:8
  273.7 0.0 slice-done
  273.7 0.0 slice-done.1
  273.7 10.3 %fusion.12 = bf16[1280,768]{1,0:T(8,128)(2,1)S(1)} fusion(bf16[1280,4096]{1,0:T(8,128)(2,1)S(1)} %bitcast.47, bf16[1,4096,768]{2,1,0:T(8,128)(2,1)S(1)} %bitcast.53, f32[1280,768]{1,0:T(8,128)} %fusion.7), kind=kOutput, calls=%fused_computation.20 | convolution fusion | flops 8058961920 | bytes 22675456 | tf_op jit(solution)/shard_map/dot_general | solution.py:9
  284.1 10.7 %convolution_convert_fusion = bf16[1280,4096]{1,0:T(8,128)(2,1)} fusion(bf16[1280,768]{1,0:T(8,128)(2,1)S(1)} %fusion.12, bf16[1,768,4096]{2,1,0:T(8,128)(2,1)S(1)} %bitcast.55), kind=kOutput, calls=%fused_computation.10 | convolution fusion | flops 8058306560 | bytes 18743296 | tf_op jit(solution)/shard_map/dot_general | solution.py:11
  294.7 5.0 all-to-all-start.1
  299.7 0.0 reduce-scatter.2.cloned.1.call-start
  299.8 14.9 %all_gather.10 = f32[1024,8]{0,1:T(8,128)S(1)} all-gather(f32[128,8]{0,1:T(8,128)S(1)} %divide_multiply_fusion), channel_id=1, replica_groups=mesh['rep'=16,'exp'=8] {'exp'}, dimensions={0}, use_global_device_ids=true | all-gather | bytes 36864 | tf_op jit(solution)/shard_map/all_gather | solution.py:41
  314.7 0.2 copy.35
  314.9 0.3 reshape.190
  315.1 30.4 %scatter_custom_fusion.2 = f32[1280]{0:T(1024)S(1)} fusion(s32[8192]{0:T(1024)S(1)} %bitcast.50, f32[8192]{0:T(1024)S(1)} %reshape.190, f32[]{:T(128)} %constant.89.clone.1), kind=kCustom, calls=%fused_computation.67 | custom fusion | bytes 5124 | tf_op jit(solution)/shard_map/scatter | solution.py:52
  345.6 126.3 %all-to-all-done.1 = bf16[16,80,4096]{2,1,0:T(8,128)(2,1)} async-done(((bf16[16,80,4096]{2,1,0:T(8,128)(2,1)}), bf16[16,80,4096]{2,1,0:T(8,128)(2,1)}, u32[]{:S(2)}, u32[]{:S(2)}) %all-to-all-start.1) | async-done | bytes 10485792 | tf_op jit(solution)/shard_map/all_to_all | solution.py:59
  471.9 42.9 %scatter_custom_fusion.3 = f32[1024,4096]{1,0:T(8,128)} fusion(s32[1280]{0:T(1024)S(1)} %get-tuple-element.8, bf16[1280,4096]{1,0:T(8,128)(2,1)} %bitcast.16, f32[1280]{0:T(1024)S(1)} %scatter_custom_fusion.2, f32[]{:T(128)} %constant.89.clone.1), kind=kCustom, calls=%fused_computation.7 | custom fusion | flops 15728640 | bytes 27271172 | tf_op jit(solution)/shard_map/scatter-add | solution.py:62
  514.8 9.0 %convert_element_type.50 = bf16[1024,4096]{1,0:T(8,128)(2,1)} convert(f32[1024,4096]{1,0:T(8,128)} %scatter_custom_fusion.3) | non-fusion elementwise | flops 4194304 | bytes 25165824 | tf_op jit(solution)/shard_map/convert_element_type | solution.py:63
  523.8 0.0 reduce-scatter.2.cloned.1.call-update
  523.8 59.5 %reduce-scatter.2.cloned.1.call-done = bf16[128,4096]{1,0:T(8,128)(2,1)} async-done(((bf16[1024,4096]{1,0:T(8,128)(2,1)}), bf16[128,4096]{1,0:T(8,128)(2,1)}) %reduce-scatter.2.cloned.1.call-update) | async-done | bytes 1048592 | tf_op jit(solution)/shard_map/reduce_scatter | solution.py:63
  (31 shorter events, 0.4 us)
Async XLA Ops:
  6.5 92.2 %all-gather.2.cloned.1.call-start = ((), (), s32[]{:S(2)}) async-start(), calls=%async_computation.3 | async-start | bytes 9437184 | tf_op jit(solution)/shard_map/all_gather | solution.py:39
  121.9 7.0 %copy-start = (f32[4096]{0:T(1024)S(1)}, f32[4096]{0:T(1024)}, u32[]{:S(2)}) copy-start(f32[4096]{0:T(1024)} %param.14) | copy-start | bytes 49156
  138.0 135.8 %slice-start = ((s8[6291456]{0:T(1024)(128)(4,1)}), s8[4194304]{0:T(1024)(128)(4,1)S(1)}, s32[]{:S(2)}) async-start(s8[6291456]{0:T(1024)(128)(4,1)} %bitcast.52), calls=%async_computation.5 | async-start | bytes 8388608
  138.0 146.1 %slice-start.2 = ((s8[6291456]{0:T(1024)(128)(4,1)}), s8[4194304]{0:T(1024)(128)(4,1)S(1)}, s32[]{:S(2)}) async-start(s8[6291456]{0:T(1024)(128)(4,1)} %bitcast.54), calls=%async_computation.7 | async-start | bytes 8388608
  261.9 11.8 %slice-start.1 = ((s8[6291456]{0:T(1024)(128)(4,1)}), s8[2097152]{0:T(1024)(128)(4,1)S(1)}, s32[]{:S(2)}) async-start(s8[6291456]{0:T(1024)(128)(4,1)} %bitcast.52), calls=%async_computation.6 | async-start | bytes 4194304
  261.9 22.2 %slice-start.3 = ((s8[6291456]{0:T(1024)(128)(4,1)}), s8[2097152]{0:T(1024)(128)(4,1)S(1)}, s32[]{:S(2)}) async-start(s8[6291456]{0:T(1024)(128)(4,1)} %bitcast.54), calls=%async_computation.8 | async-start | bytes 4194304
  294.7 5.0 copy-start.1
  294.7 177.1 %all-to-all-start.1 = ((bf16[16,80,4096]{2,1,0:T(8,128)(2,1)}), bf16[16,80,4096]{2,1,0:T(8,128)(2,1)}, u32[]{:S(2)}, u32[]{:S(2)}) async-start(bf16[16,80,4096]{2,1,0:T(8,128)(2,1)} %bitcast.45), calls=%async_computation.1 | async-start | bytes 20971520 | tf_op jit(solution)/shard_map/all_to_all | solution.py:59
  299.7 283.6 %reduce-scatter.2.cloned.1.call-start = ((), (), s32[]{:S(2)}) async-start(), calls=%async_computation.4 | async-start | bytes 9437184 | tf_op jit(solution)/shard_map/reduce_scatter | solution.py:63
Sparse Core Ops, SparseCore 0:
  9.1 53.5 all-gather.1
  523.9 59.3 reduce-scatter.1
where the time goes:
time: 597 us; the launch traced here: 590 us
  waiting for transfers between devices  187 us (31%)
  blocking collectives  154 us (26%)
  local copies, waits for them, and re-layouts  127 us (21%)
  other arithmetic  70.3 us (12%)
  matrix products  32.8 us (5%)
  between operations  14.6 us (2%)
    all_to_all x1, waiting for transfers between devices, shards(): lax.all_to_all(results, 'rep', split_axis=0, concat_axis=0, tiled=True)  126 us
    all_to_all x1, blocking collectives, shards(): lax.all_to_all(outgoing, 'rep', split_axis=0, concat_axis=0, tiled=True)  124 us
    reduce_scatter x1, waiting for transfers between devices, shards(): lax.psum_scatter(partial.astype(jnp.bfloat16), 'exp', scatter_dimension=0...  59.5 us
    scatter-add x1, other arithmetic, shards(): jnp.zeros((micro, width), jnp.float32).at[target].add(contrib, mode='drop')  42.9 us
    scatter x1, local copies, waits for them, and re-layouts, shards(): filled = jnp.zeros((slots,), jnp.bool_).at[dest].set(True, mode='drop')  34.6 us
    scatter x1, local copies, waits for them, and re-layouts, shards(): src_row = jnp.zeros((slots,), jnp.int32).at[dest].set(row_id, mode='drop')  30.9 us
    scatter x1, local copies, waits for them, and re-layouts, shards(): jnp.zeros((slots,), jnp.float32).at[dest]  30.4 us
    gather x1, local copies, waits for them, and re-layouts, shards(): jnp.take(group, jnp.take(parent_all, src_row), axis=0).astype(jnp.float32)  23.2 us
  transfers between devices with their start and end apart: 3, of which 2 were waited for; matrix products, arithmetic and copies ran while one was open for 18% of the time, Pallas kernels for 0%

commit v1 on v0

--- a/solution.py
+++ b/solution.py
@@ -38,7 +38,9 @@
     )
     group = lax.all_gather(hidden, "exp", axis=0, tiled=True)
     ints_all = lax.all_gather(ints, "exp", axis=0, tiled=True)
-    w_all = lax.all_gather(weights, "exp", axis=0, tiled=True)
+    w_all = jnp.concatenate(
+        lax.all_to_all(jnp.stack([weights] * lax.axis_size("exp")), "exp", 0, 0), axis=0
+    )
     code_all = ints_all[:, :top]
     rank_all = ints_all[:, top : 2 * top]
     parent_all = ints_all[:, 2 * top]

time: 597 us -> 688 us (1.15)
  waiting for transfers between devices: 187 us -> 389 us
  blocking collectives: 154 us -> 15.3 us
  starting transfers between devices: 5.02 us -> 22.6 us
    all_to_all x0 -> x2, waiting for transfers between devices: none -> 180 us  [the longest x1 180 us: shards(): lax.all_to_all(outgoing, 'rep', split_axis=0, concat_axis=0, tiled=True)]
    all_to_all x1 -> x0, blocking collectives: 124 us -> none  [shards(): lax.all_to_all(outgoing, 'rep', split_axis=0, concat_axis=0, tiled=True)]
    all_to_all x1, waiting for transfers between devices: 126 us -> 151 us  [shards(): lax.all_to_all(results, 'rep', split_axis=0, concat_axis=0, tiled=True)]
    all_gather x1 -> x0, blocking collectives: 14.9 us -> none  [shards(): w_all = lax.all_gather(weights, 'exp', axis=0, tiled=True)]
    all_to_all x0 -> x2, starting transfers between devices: none -> 12.2 us  [the longest x1 6.93 us: shards(): lax.all_to_all(outgoing, 'rep', split_axis=0, concat_axis=0, tiled=True)]
  transfers between devices with their start and end apart: 3 -> 5, of which waited for: 2 -> 3; matrix products, arithmetic and copies ran while one was open for 18% -> 21% of each run, Pallas kernels for 0% -> 0%
where the time goes in v1:
time: 688 us; the launch traced here: 681 us
  waiting for transfers between devices  389 us (57%)
  local copies, waits for them, and re-layouts  128 us (19%)
  other arithmetic  73.1 us (11%)
  matrix products  38.8 us (6%)
  starting transfers between devices  22.6 us (3%)
  blocking collectives  15.3 us (2%)
  between operations  14.5 us (2%)
    all_to_all x1, waiting for transfers between devices, shards(): lax.all_to_all(outgoing, 'rep', split_axis=0, concat_axis=0, tiled=True)  180 us
    all_to_all x1, waiting for transfers between devices, shards(): lax.all_to_all(results, 'rep', split_axis=0, concat_axis=0, tiled=True)  151 us
    reduce_scatter x1, waiting for transfers between devices, shards(): lax.psum_scatter(partial.astype(jnp.bfloat16), 'exp', scatter_dimension=0...  57.8 us
    scatter-add x1, other arithmetic, shards(): jnp.zeros((micro, width), jnp.float32).at[target].add(contrib, mode='drop')  42.9 us
    scatter x1, local copies, waits for them, and re-layouts, shards(): filled = jnp.zeros((slots,), jnp.bool_).at[dest].set(True, mode='drop')  34.6 us
    scatter x1, local copies, waits for them, and re-layouts, shards(): src_row = jnp.zeros((slots,), jnp.int32).at[dest].set(row_id, mode='drop')  30.9 us
    scatter x1, local copies, waits for them, and re-layouts, shards(): jnp.zeros((slots,), jnp.float32).at[dest]  30.4 us
    gather x1, local copies, waits for them, and re-layouts, shards(): jnp.take(group, jnp.take(parent_all, src_row), axis=0).astype(jnp.float32)  23.2 us
  transfers between devices with their start and end apart: 5, of which 3 were waited for; matrix products, arithmetic and copies ran while one was open for 21% of the time, Pallas kernels for 0%

profile of v1, /device:TPU:1, one launch (start us, length us, event | category | flops | bytes accessed | tf_op | source)
XLA Modules:
  0.0 680.9 jit_solution(4872146271243257777)
XLA Ops:
  6.5 0.0 all-gather.2.cloned.1.call-start
  6.5 0.7 all-gather.2.cloned.1.call-update
  7.3 0.8 copy.29
  8.0 0.1 eq.37
  8.1 0.1 eq.33
  8.9 0.1 broadcast_in_dim.94.clone
  9.0 0.1 and.55
  9.1 0.1 copy.32
  9.2 0.3 fusion.17
  9.7 0.1 copy.33
  9.8 0.5 fusion.16
  10.3 0.1 reshape.148
  10.4 0.7 broadcast_select_fusion
  11.1 0.7 pad_add_fusion
  11.8 15.3 %all_gather.6 = s32[1024,17]{0,1:T(8,128)S(1)} all-gather(s32[128,17]{0,1:T(8,128)S(1)} %pad_add_fusion), channel_id=1, replica_groups=mesh['rep'=16,'exp'=8] {'exp'}, dimensions={0}, use_global_device_ids=true | all-gather | bytes 78336 | tf_op jit(solution)/shard_map/all_gather | solution.py:40
  27.1 0.2 copy.35
  27.3 0.3 reshape.149
  27.7 34.6 %scatter_custom_fusion = pred[1280]{0:T(1024)(128)(4,1)S(1)} fusion(s32[8192]{0:T(1024)S(1)} %bitcast.45, pred[8192]{0:T(1024)(128)(4,1)S(1)} %broadcast.151, pred[]{:T(512)} %constant.90.clone.1), kind=kCustom, calls=%fused_computation.72 | custom fusion | bytes 1281 | tf_op jit(solution)/shard_map/scatter | solution.py:53
  62.3 0.1 broadcast_in_dim.105
  62.4 0.3 reshape.180
  62.7 30.9 %scatter_custom_fusion.1 = s32[1280]{0:T(1024)S(1)} fusion(s32[8192]{0:T(1024)S(1)} %bitcast.46, s32[8192]{0:T(1024)S(1)} %reshape.180, s32[]{:T(128)} %constant.93.clone.1), kind=kCustom, calls=%fused_computation.69 | custom fusion | bytes 5124 | tf_op jit(solution)/shard_map/scatter | solution.py:52
  93.6 5.0 gather_fusion
  98.6 0.1 broadcast_in_dim.109
  98.7 0.0 all-gather.2.cloned.1.call-done
  98.7 23.2 %gather_fusion.1 = bf16[1280,4096]{1,0:T(8,128)(2,1)} fusion(bf16[1024,4096]{1,0:T(8,128)(2,1)} %all-gather.2.cloned.1.call-done, s32[2048]{0:T(1024)S(1)} %pad_clamp_fusion), kind=kCustom, calls=%fused_computation.1 | custom fusion | bytes 20976640 | tf_op jit(solution)/shard_map/jit(_take)/gather | solution.py:55
  121.9 6.9 %multiply_reduce_fusion = f32[1280]{0:T(1024)S(1)} fusion(bf16[1280,4096]{1,0:T(8,128)(2,1)} %gather_fusion.1, pred[1280]{0:T(1024)(128)(4,1)S(1)} %get-tuple-element.5), kind=kLoop, calls=%fused_computation.9 | loop fusion | flops 20970240 | bytes 10492160 | tf_op jit(solution)/shard_map/reduce_sum | solution.py:56
  128.8 0.1 rsqrt.12
  128.9 0.0 copy-done
  128.9 11.9 %fusion.1 = bf16[16,80,4096]{2,1,0:T(8,128)(2,1)} fusion(f32[4096]{0:T(1024)S(1)} %copy-done, f32[16,80]{1,0:T(8,128)S(1)} %rsqrt.12, bf16[16,80,4096]{2,1,0:T(8,128)(2,1)} %bitcast.43, pred[16,80]{1,0:T(8,128)(4,1)S(1)} %broadcast_in_dim.109, pred[16,80]{1,0:T(8,128)(4,1)S(1)} %broadcast_in_dim.105), kind=kLoop, calls=%fused_computation.11 | loop fusion | flops 31457280 | bytes 20995584 | tf_op jit(solution)/shard_map/jit(_where)/select_n | solution.py:58
  140.8 6.9 %all-to-all-start.1 = ((bf16[16,80,4096]{2,1,0:T(8,128)(2,1)}), bf16[16,80,4096]{2,1,0:T(8,128)(2,1)}, u32[]{:S(2)}, u32[]{:S(2)}) async-start(bf16[16,80,4096]{2,1,0:T(8,128)(2,1)} %fusion.1), calls=%async_computation.1 | async-start | bytes 20971520 | tf_op jit(solution)/shard_map/all_to_all | solution.py:59
  147.7 0.0 copy-done.1
  147.8 179.5 %all-to-all-done.1 = bf16[16,80,4096]{2,1,0:T(8,128)(2,1)} async-done(((bf16[16,80,4096]{2,1,0:T(8,128)(2,1)}), bf16[16,80,4096]{2,1,0:T(8,128)(2,1)}, u32[]{:S(2)}, u32[]{:S(2)}) %all-to-all-start.1) | async-done | bytes 10485792 | tf_op jit(solution)/shard_map/all_to_all | solution.py:59
  327.3 0.6 stack.2
  327.9 5.3 all-to-all-start
  333.2 12.1 %fusion.7 = f32[1280,768]{1,0:T(8,128)S(1)} fusion(bf16[1280,4096]{1,0:T(8,128)(2,1)} %bitcast.9, bf16[1,4096,768]{2,1,0:T(8,128)(2,1)} %param.15), kind=kOutput, calls=%fused_computation.17 | convolution fusion | flops 8053063680 | bytes 20709376 | tf_op jit(solution)/shard_map/dot_general | solution.py:8
  345.3 13.1 %fusion.12 = bf16[1280,768]{1,0:T(8,128)(2,1)S(1)} fusion(bf16[1280,4096]{1,0:T(8,128)(2,1)} %bitcast.9, bf16[1,4096,768]{2,1,0:T(8,128)(2,1)} %param.16, f32[1280,768]{1,0:T(8,128)S(1)} %fusion.7), kind=kOutput, calls=%fused_computation.20 | convolution fusion | flops 8058961920 | bytes 22675456 | tf_op jit(solution)/shard_map/dot_general | solution.py:9
  358.4 13.5 %convolution_convert_fusion = bf16[1280,4096]{1,0:T(8,128)(2,1)} fusion(bf16[1280,768]{1,0:T(8,128)(2,1)S(1)} %fusion.12, bf16[1,768,4096]{2,1,0:T(8,128)(2,1)} %param.17), kind=kOutput, calls=%fused_computation.10 | convolution fusion | flops 8058306560 | bytes 18743296 | tf_op jit(solution)/shard_map/dot_general | solution.py:11
  372.0 0.0 all-to-all-done
  372.0 10.3 %all-to-all-start.2 = ((bf16[16,80,4096]{2,1,0:T(8,128)(2,1)}), bf16[16,80,4096]{2,1,0:T(8,128)(2,1)}, u32[]{:S(2)}, u32[]{:S(2)}) async-start(bf16[16,80,4096]{2,1,0:T(8,128)(2,1)} %bitcast.44), calls=%async_computation.2 | async-start | bytes 20971520 | tf_op jit(solution)/shard_map/all_to_all | solution.py:61
  382.3 0.0 reduce-scatter.2.cloned.1.call-start
  382.3 0.2 copy.36
  382.5 0.3 reshape.188
  382.8 30.4 %scatter_custom_fusion.2 = f32[1280]{0:T(1024)S(1)} fusion(s32[8192]{0:T(1024)S(1)} %bitcast.47, f32[8192]{0:T(1024)S(1)} %reshape.188, f32[]{:T(128)} %constant.89.clone.1), kind=kCustom, calls=%fused_computation.67 | custom fusion | bytes 5124 | tf_op jit(solution)/shard_map/scatter | solution.py:54
  413.3 150.8 %all-to-all-done.2 = bf16[16,80,4096]{2,1,0:T(8,128)(2,1)} async-done(((bf16[16,80,4096]{2,1,0:T(8,128)(2,1)}), bf16[16,80,4096]{2,1,0:T(8,128)(2,1)}, u32[]{:S(2)}, u32[]{:S(2)}) %all-to-all-start.2) | async-done | bytes 10485792 | tf_op jit(solution)/shard_map/all_to_all | solution.py:61
  564.1 42.9 %scatter_custom_fusion.3 = f32[1024,4096]{1,0:T(8,128)} fusion(s32[1280]{0:T(1024)S(1)} %get-tuple-element.8, bf16[1280,4096]{1,0:T(8,128)(2,1)} %bitcast.16, f32[1280]{0:T(1024)S(1)} %scatter_custom_fusion.2, f32[]{:T(128)} %constant.89.clone.1), kind=kCustom, calls=%fused_computation.7 | custom fusion | flops 15728640 | bytes 27271172 | tf_op jit(solution)/shard_map/scatter-add | solution.py:64
  606.9 9.0 %convert_element_type.50 = bf16[1024,4096]{1,0:T(8,128)(2,1)} convert(f32[1024,4096]{1,0:T(8,128)} %scatter_custom_fusion.3) | non-fusion elementwise | flops 4194304 | bytes 25165824 | tf_op jit(solution)/shard_map/convert_element_type | solution.py:65
  616.0 0.0 reduce-scatter.2.cloned.1.call-update
  616.0 57.8 %reduce-scatter.2.cloned.1.call-done = bf16[128,4096]{1,0:T(8,128)(2,1)} async-done(((bf16[1024,4096]{1,0:T(8,128)(2,1)}), bf16[128,4096]{1,0:T(8,128)(2,1)}) %reduce-scatter.2.cloned.1.call-update) | async-done | bytes 1048592 | tf_op jit(solution)/shard_map/reduce_scatter | solution.py:65
  (23 shorter events, 0.4 us)
Async XLA Ops:
  6.5 92.2 %all-gather.2.cloned.1.call-start = ((), (), s32[]{:S(2)}) async-start(), calls=%async_computation.4 | async-start | bytes 9437184 | tf_op jit(solution)/shard_map/all_gather | solution.py:39
  121.9 7.0 %copy-start = (f32[4096]{0:T(1024)S(1)}, f32[4096]{0:T(1024)}, u32[]{:S(2)}) copy-start(f32[4096]{0:T(1024)} %param.14) | copy-start | bytes 49156
  140.8 6.9 %copy-start.1 = (f32[128,8]{0,1:T(8,128)S(1)}, f32[128,8]{0,1:T(8,128)}, u32[]{:S(2)}) copy-start(f32[128,8]{0,1:T(8,128)} %param.12) | copy-start | bytes 12292
  140.8 186.5 %all-to-all-start.1 = ((bf16[16,80,4096]{2,1,0:T(8,128)(2,1)}), bf16[16,80,4096]{2,1,0:T(8,128)(2,1)}, u32[]{:S(2)}, u32[]{:S(2)}) async-start(bf16[16,80,4096]{2,1,0:T(8,128)(2,1)} %fusion.1), calls=%async_computation.1 | async-start | bytes 20971520 | tf_op jit(solution)/shard_map/all_to_all | solution.py:59
  327.9 44.1 %all-to-all-start = ((f32[8,128,8]{1,2,0:T(8,128)}), f32[8,128,8]{1,2,0:T(8,128)S(1)}, u32[]{:S(2)}, u32[]{:S(2)}) async-start(f32[8,128,8]{1,2,0:T(8,128)} %stack.2), calls=%async_computation | async-start | bytes 65536 | tf_op jit(solution)/shard_map/all_to_all | solution.py:42
  372.0 192.1 %all-to-all-start.2 = ((bf16[16,80,4096]{2,1,0:T(8,128)(2,1)}), bf16[16,80,4096]{2,1,0:T(8,128)(2,1)}, u32[]{:S(2)}, u32[]{:S(2)}) async-start(bf16[16,80,4096]{2,1,0:T(8,128)(2,1)} %bitcast.44), calls=%async_computation.2 | async-start | bytes 20971520 | tf_op jit(solution)/shard_map/all_to_all | solution.py:61
  382.3 291.5 %reduce-scatter.2.cloned.1.call-start = ((), (), s32[]{:S(2)}) async-start(), calls=%async_computation.5 | async-start | bytes 9437184 | tf_op jit(solution)/shard_map/reduce_scatter | solution.py:65
Sparse Core Ops, SparseCore 0:
  9.1 53.5 all-gather.1
  616.1 57.6 reduce-scatter.1
